TPU v7x, 256 devices: a whole 4x4x8 slice. The times are simulated.
256 devices in a mesh: fsdp: 32 (over z_hi, y, core), tp: 8 (over z_lo, x).
Axes of the slice: x: 4, y: 4, z: 8 (z_hi: 4, z_lo: 2; z = z_hi * 2 + z_lo), core: 2. Of those that a mesh axis runs over, the one named last changes fastest.
Arguments:
- normed: bfloat16 [32768, 8192], P('fsdp'), may hold values from -6 to 6
- kv_weight: bfloat16 [8192, 2048], P('fsdp', 'tp'), may hold values from -0.0625 to 0.0625
- kv_cotangent: bfloat16 [32768, 2048], P('fsdp', 'tp'), may hold values from -0.25 to 0.25
- first_moment: float32 [8192, 2048], P('fsdp', 'tp'), may hold values from -6 to 6
- second_moment: float32 [8192, 2048], P('fsdp', 'tp'), may hold values from 0.5 to 5
- cauchy_points: int32 [20], replicated, may hold values from 0 to 19, each once
Outputs:
- keys_values: bfloat16 [32768, 2048], P('fsdp', 'tp')
- new_first: float32 [8192, 2048], P('fsdp', 'tp')
- new_second: float32 [8192, 2048], P('fsdp', 'tp')
- parity: float32 [4, 2, 4096, 256], P(None, None, 'fsdp', 'tp')
Inputs may be any that keep to these rules, and one draw needn't show every extreme that they name: `cauchy_points`: each value once; the first 4 entries are the parity points, the other 16 the members' points in rank order.
All inputs are finite; a program needn't handle non-finite values.
Results may differ from a plain program's by a relative error of at most 0.001.
Values may be sent and summed in bfloat16 or wider, within the bound.
A program may use at most 192 MiB of HBM per device.

v0:
```python
import jax
import jax.numpy as jnp
from jax import lax
from jax.sharding import PartitionSpec as P

GROUP = 16
PARITY = 4
beta_first = 0.9
beta_second = 0.95


def from_partner(shard, axis, bit):
    return lax.ppermute(shard, axis, [(i, i ^ 1 << bit) for i in range(lax.axis_size(axis))])


def halve_rows(values, fsdp_index):
    half_rows = values.shape[2] // 2
    upper = fsdp_index // (1 << 0) % 2
    retained = lax.dynamic_slice_in_dim(values, upper * half_rows, half_rows, 2)
    outgoing = lax.dynamic_slice_in_dim(values, (1 - upper) * half_rows, half_rows, 2)
    values = retained + from_partner(outgoing, "fsdp", 0)
    return values


def local(normed, kv_weight, kv_cotangent, first_moment, second_moment, cauchy_points):
    contract = (((0,), (0,)), ((), ()))
    columns = normed
    projected = jnp.dot(
        columns,
        lax.all_gather(kv_weight, "fsdp", axis=0, tiled=True),
        preferred_element_type=jnp.float32,
    )
    keys_values = projected.astype(jnp.bfloat16)
    columns = normed
    gradient = lax.psum_scatter(
        lax.dot_general(columns, kv_cotangent, contract, preferred_element_type=jnp.float32),
        "fsdp",
        scatter_dimension=0,
        tiled=True,
    )
    new_first = beta_first * first_moment + (1.0 - beta_first) * gradient
    new_second = beta_second * second_moment + (1.0 - beta_second) * gradient * gradient
    points = cauchy_points.astype(jnp.float32)
    cauchy = 1.0 / (points[:PARITY, None] - points[None, PARITY:])
    tp_count = lax.axis_size("tp")
    group_rows = GROUP // tp_count
    fsdp_index = lax.axis_index("fsdp")
    payload = jnp.stack([new_first, new_second])
    member_rank = fsdp_index % group_rows * tp_count + lax.axis_index("tp")
    selector = (jnp.arange(GROUP, dtype=jnp.int32) == member_rank).astype(jnp.float32)
    column_weights = jnp.sum(cauchy * selector[None, :], axis=1)
    contribution = column_weights[:, None, None, None] * payload[None]
    summed = lax.psum_scatter(contribution, "tp", scatter_dimension=3, tiled=True)
    parity = halve_rows(summed, fsdp_index)
    return (keys_values, new_first, new_second, parity)


def solution(mesh):
    return jax.shard_map(
        local,
        mesh=mesh,
        in_specs=(
            P("fsdp", None),
            P("fsdp", "tp"),
            P("fsdp", "tp"),
            P("fsdp", "tp"),
            P("fsdp", "tp"),
            P(),
        ),
        out_specs=(P("fsdp", "tp"), P("fsdp", "tp"), P("fsdp", "tp"), P(None, None, "fsdp", "tp")),
        check_vma=False,
    )
```

profile of v0, /device:TPU:1, one launch (start us, length us, event | category | flops | bytes accessed | tf_op | source)
XLA Modules:
  0.0 275.5 jit_solution(3754259046699484786)
XLA Ops:
  7.2 0.0 copy-start
  7.2 0.0 reduce-scatter.3.cloned.1.call-start
  7.2 1.0 copy-done
  8.2 13.7 %fusion.1 = f32[8192,256]{1,0:T(8,128)} fusion(bf16[1024,8192]{1,0:T(8,128)(2,1)} %param.6, bf16[1024,256]{1,0:T(8,128)(2,1)S(1)} %copy-done), kind=kOutput, calls=%fused_computation.10 | convolution fusion | flops 4294967296 | bytes 25690112 | tf_op jit(solution)/shard_map/dot_general | solution.py:36
  22.0 0.0 reduce-scatter.3.cloned.1.call-update
  22.0 0.0 reduce-scatter.5.cloned.1.call-start
  22.0 0.6 copy-done.6
  22.6 0.1 slice.7
  22.7 0.2 multiply_reduce_fusion
  22.9 123.0 %reduce-scatter.3.cloned.1.call-done = f32[256,256]{1,0:T(8,128)} async-done(((f32[8192,256]{1,0:T(8,128)}), f32[256,256]{1,0:T(8,128)}) %reduce-scatter.3.cloned.1.call-update) | async-done | bytes 262160 | tf_op jit(solution)/shard_map/reduce_scatter | solution.py:35
  145.9 1.0 fusion
  146.9 0.0 copy-start.1
  146.9 0.0 copy-start.2
  147.0 0.2 copy.11
  147.2 1.6 broadcast_multiply_fusion
  148.8 0.0 reduce-scatter.5.cloned.1.call-update
  148.8 0.0 all-gather.2.cloned.1.call-start
  148.8 0.7 all-gather.2.cloned.1.call-update
  149.5 39.2 %reduce-scatter.5.cloned.1.call-done = f32[4,2,256,32]{2,3,1,0:T(8,128)} async-done(((f32[4,2,256,256]{2,3,1,0:T(8,128)}), f32[4,2,256,32]{2,3,1,0:T(8,128)}) %reduce-scatter.5.cloned.1.call-update) | async-done | bytes 262160 | tf_op jit(solution)/shard_map/reduce_scatter | solution.py:53
  188.7 0.9 constant_dynamic-slice_fusion
  189.7 5.9 %collective-permute-start = (f32[4,2,128,32]{2,3,1,0:T(8,128)S(1)}, f32[4,2,128,32]{2,3,1,0:T(8,128)S(1)}, u32[]{:S(2)}, u32[]{:S(2)}) collective-permute-start(f32[4,2,128,32]{2,3,1,0:T(8,128)S(1)} %constant_dynamic-slice_fusion), channel_id=1, source_target_pairs={{0,8},{8,0},{16,24},{24,16},{32,40},{40,32},{48,56},{56,48},{64,72... | collective-permute-start | bytes 393224 | tf_op jit(solution)/shard_map/ppermute | solution.py:13
  195.6 60.5 %all-gather.2.cloned.1.call-done = bf16[8192,256]{1,0:T(8,128)(2,1)} async-done(((bf16[256,256]{1,0:T(8,128)(2,1)}), bf16[8192,256]{1,0:T(8,128)(2,1)}) %all-gather.2.cloned.1.call-update) | async-done | bytes 4194320 | tf_op jit(solution)/shard_map/all_gather | solution.py:30
  256.0 12.2 %convolution_convert_fusion = bf16[1024,256]{1,0:T(8,128)(2,1)} fusion(bf16[1024,8192]{1,0:T(8,128)(2,1)} %param.6, bf16[8192,256]{1,0:T(8,128)(2,1)} %all-gather.2.cloned.1.call-done), kind=kOutput, calls=%fused_computation | convolution fusion | flops 4295229440 | bytes 21495808 | tf_op jit(solution)/shard_map/dot_general | solution.py:28
  268.3 0.7 dynamic-slice_add_fusion
  (13 shorter events, 0.1 us)
Async XLA Ops:
  7.2 1.0 copy-start
  7.2 138.7 %reduce-scatter.3.cloned.1.call-start = ((), (), s32[]{:S(2)}) async-start(), calls=%async_computation.3 | async-start | bytes 8650752 | tf_op jit(solution)/shard_map/reduce_scatter | solution.py:35
  22.0 0.7 copy-start.6
  22.0 123.9 %copy-start.3 = (f32[256,256]{1,0:T(8,128)S(1)}, f32[256,256]{1,0:T(8,128)}, u32[]{:S(2)}) copy-start(f32[256,256]{1,0:T(8,128)} %param.10) | copy-start | bytes 786436
  22.0 123.9 %copy-start.4 = (f32[256,256]{1,0:T(8,128)S(1)}, f32[256,256]{1,0:T(8,128)}, u32[]{:S(2)}) copy-start(f32[256,256]{1,0:T(8,128)} %param.9) | copy-start | bytes 786436
  22.0 166.7 %reduce-scatter.5.cloned.1.call-start = ((), (), s32[]{:S(2)}) async-start(), calls=%async_computation.4 | async-start | bytes 2359296 | tf_op jit(solution)/shard_map/reduce_scatter | solution.py:53
  146.9 121.3 %copy-start.1 = (f32[256,256]{1,0:T(8,128)}, f32[256,256]{1,0:T(8,128)S(1)}, u32[]{:S(2)}) copy-start(f32[256,256]{1,0:T(8,128)S(1)} %get-tuple-element.4) | copy-start | bytes 786436
  146.9 121.3 %copy-start.2 = (f32[256,256]{1,0:T(8,128)}, f32[256,256]{1,0:T(8,128)S(1)}, u32[]{:S(2)}) copy-start(f32[256,256]{1,0:T(8,128)S(1)} %get-tuple-element.5) | copy-start | bytes 786436
  148.8 107.2 %all-gather.2.cloned.1.call-start = ((), (), s32[]{:S(2)}) async-start(), calls=%async_computation.2 | async-start | bytes 4325376 | tf_op jit(solution)/shard_map/all_gather | solution.py:30
  189.6 78.6 %copy-start.5 = (f32[4,2,256,32]{2,3,1,0:T(8,128)S(1)}, f32[4,2,256,32]{2,3,1,0:T(8,128)}, u32[]{:S(2)}) copy-start(f32[4,2,256,32]{2,3,1,0:T(8,128)} %reduce-scatter.5.cloned.1.call-done) | copy-start | bytes 786436
  189.7 78.6 %collective-permute-start = (f32[4,2,128,32]{2,3,1,0:T(8,128)S(1)}, f32[4,2,128,32]{2,3,1,0:T(8,128)S(1)}, u32[]{:S(2)}, u32[]{:S(2)}) collective-permute-start(f32[4,2,128,32]{2,3,1,0:T(8,128)S(1)} %constant_dynamic-slice_fusion), channel_id=1, source_target_pairs={{0,8},{8,0},{16,24},{24,16},{32,40},{40,32},{48,56},{56,48},{64,72... | collective-permute-start | bytes 393224 | tf_op jit(solution)/shard_map/ppermute | solution.py:13
Sparse Core Ops, SparseCore 0:
  22.1 123.7 reduce-scatter.2
  148.9 39.7 reduce-scatter.4
  191.3 64.6 all-gather.1
where the time goes:
time: 276 us; the launch traced here: 275 us
  waiting for transfers between devices  223 us (81%)
  matrix products  26 us (9%)
  between operations  13.8 us (5%)
  starting transfers between devices  6.01 us (2%)
  other arithmetic  3.5 us (1%)
  local copies, waits for them, and re-layouts  2.77 us (1%)
    reduce_scatter x1, waiting for transfers between devices, local(): lax.psum_scatter(lax.dot_general(columns, kv_cotangent, contract, preferr...  123 us
    all_gather x1, waiting for transfers between devices, local(): lax.all_gather(kv_weight, 'fsdp', axis=0, tiled=True)  60.5 us
    reduce_scatter x1, waiting for transfers between devices, local(): lax.psum_scatter(contribution, 'tp', scatter_dimension=3, tiled=True)  39.2 us
    dot_general x1, matrix products, local(): lax.dot_general(columns, kv_cotangent, contract, preferred_element_type=j...  13.7 us
    dot_general x1, matrix products, local(): jnp.dot(columns, lax.all_gather(kv_weight, 'fsdp', axis=0, tiled=True), p...  12.2 us
    ppermute x1, starting transfers between devices, from_partner(): lax.ppermute(shard, axis, [(i, i ^ 1 << bit) for i in range(lax.axis_size...  5.89 us
  transfers between devices with their start and end apart: 4, of which 3 were waited for; matrix products, arithmetic and copies ran while one was open for 5% of the time, Pallas kernels for 0%

commit v1 on v0

--- a/solution.py
+++ b/solution.py
@@ -27,7 +27,9 @@
     columns = normed
     projected = jnp.dot(
         columns,
-        lax.all_gather(kv_weight, "fsdp", axis=0, tiled=True),
+        jnp.concatenate(
+            lax.all_to_all(jnp.stack([kv_weight] * lax.axis_size("fsdp")), "fsdp", 0, 0), axis=0
+        ),
         preferred_element_type=jnp.float32,
     )
     keys_values = projected.astype(jnp.bfloat16)

time: 276 us -> 262 us (0.949)
  waiting for transfers between devices: 223 us -> 194 us
  starting transfers between devices: 6.01 us -> 18.8 us
    all_gather x1 -> x0, waiting for transfers between devices: 60.5 us -> none  [local(): lax.all_gather(kv_weight, 'fsdp', axis=0, tiled=True)]
    reduce_scatter x1, waiting for transfers between devices: 123 us -> 154 us  [local(): lax.psum_scatter(lax.dot_general(columns, kv_cotangent, contract, preferr...]
    all_to_all x0 -> x1, starting transfers between devices: none -> 12.8 us  [local(): lax.all_to_all(jnp.stack([kv_weight] * lax.axis_size('fsdp')), 'fsdp', 0, 0)]
  transfers between devices with their start and end apart: 4 -> 4, of which waited for: 3 -> 2; matrix products, arithmetic and copies ran while one was open for 5% -> 7% of each run, Pallas kernels for 0% -> 0%
where the time goes in v1:
time: 262 us
  waiting for transfers between devices  194 us (74%)
  matrix products  26 us (10%)
  starting transfers between devices  18.8 us (7%)
  between operations  14.1 us (5%)
  local copies, waits for them, and re-layouts  5.48 us (2%)
  other arithmetic  3.52 us (1%)
    reduce_scatter x1, waiting for transfers between devices, local(): lax.psum_scatter(lax.dot_general(columns, kv_cotangent, contract, preferr...  154 us
    reduce_scatter x1, waiting for transfers between devices, local(): lax.psum_scatter(contribution, 'tp', scatter_dimension=3, tiled=True)  39.9 us
    dot_general x1, matrix products, local(): lax.dot_general(columns, kv_cotangent, contract, preferred_element_type=j...  13.7 us
    all_to_all x1, starting transfers between devices, local(): lax.all_to_all(jnp.stack([kv_weight] * lax.axis_size('fsdp')), 'fsdp', 0, 0)  12.8 us
    dot_general x1, matrix products, local(): jnp.dot(columns, jnp.concatenate(lax.all_to_all(jnp.stack([kv_weight] * l...  12.3 us
    ppermute x1, starting transfers between devices, from_partner(): lax.ppermute(shard, axis, [(i, i ^ 1 << bit) for i in range(lax.axis_size...  5.89 us
  transfers between devices with their start and end apart: 4, of which 2 were waited for; matrix products, arithmetic and copies ran while one was open for 7% of the time, Pallas kernels for 0%

profile of v1, /device:TPU:1, one launch (start us, length us, event | category | flops | bytes accessed | tf_op | source)
XLA Modules:
  0.0 262.1 jit_solution(5918644207596438836)
XLA Ops:
  7.2 0.0 copy-start
  7.2 0.0 reduce-scatter.3.cloned.1.call-start
  7.2 1.0 copy-done
  8.2 13.7 %fusion.1 = f32[8192,256]{1,0:T(8,128)} fusion(bf16[1024,8192]{1,0:T(8,128)(2,1)} %param.6, bf16[1024,256]{1,0:T(8,128)(2,1)S(1)} %copy-done), kind=kOutput, calls=%fused_computation.10 | convolution fusion | flops 4294967296 | bytes 25690112 | tf_op jit(solution)/shard_map/dot_general | solution.py:38
  22.0 0.0 reduce-scatter.3.cloned.1.call-update
  22.0 0.9 copy-done.6
  22.9 2.4 stack.8
  25.3 12.8 %all-to-all-start = ((bf16[32,256,256]{2,1,0:T(8,128)(2,1)}), bf16[32,256,256]{2,1,0:T(8,128)(2,1)}, u32[]{:S(2)}, u32[]{:S(2)}) async-start(bf16[32,256,256]{2,1,0:T(8,128)(2,1)} %stack.8), calls=%async_computation | async-start | bytes 8388608 | tf_op jit(solution)/shard_map/all_to_all | solution.py:31
  38.1 0.0 reduce-scatter.5.cloned.1.call-start
  38.2 0.1 slice.7
  38.2 0.2 multiply_reduce_fusion
  38.4 154.3 %reduce-scatter.3.cloned.1.call-done = f32[256,256]{1,0:T(8,128)} async-done(((f32[8192,256]{1,0:T(8,128)}), f32[256,256]{1,0:T(8,128)}) %reduce-scatter.3.cloned.1.call-update) | async-done | bytes 262160 | tf_op jit(solution)/shard_map/reduce_scatter | solution.py:37
  192.7 1.0 fusion
  193.7 0.0 copy-start.1
  193.8 0.0 copy-start.2
  193.8 0.2 copy.11
  194.0 1.6 broadcast_multiply_fusion
  195.6 0.0 reduce-scatter.5.cloned.1.call-update
  195.6 39.9 %reduce-scatter.5.cloned.1.call-done = f32[4,2,256,32]{2,3,1,0:T(8,128)} async-done(((f32[4,2,256,256]{2,3,1,0:T(8,128)}), f32[4,2,256,32]{2,3,1,0:T(8,128)}) %reduce-scatter.5.cloned.1.call-update) | async-done | bytes 262160 | tf_op jit(solution)/shard_map/reduce_scatter | solution.py:55
  235.5 0.9 constant_dynamic-slice_fusion
  236.4 5.9 %collective-permute-start = (f32[4,2,128,32]{2,3,1,0:T(8,128)S(1)}, f32[4,2,128,32]{2,3,1,0:T(8,128)S(1)}, u32[]{:S(2)}, u32[]{:S(2)}) collective-permute-start(f32[4,2,128,32]{2,3,1,0:T(8,128)S(1)} %constant_dynamic-slice_fusion), channel_id=1, source_target_pairs={{0,8},{8,0},{16,24},{24,16},{32,40},{40,32},{48,56},{56,48},{64,72... | collective-permute-start | bytes 393224 | tf_op jit(solution)/shard_map/ppermute | solution.py:13
  242.3 0.0 all-to-all-done
  242.3 12.3 %convolution_convert_fusion = bf16[1024,256]{1,0:T(8,128)(2,1)} fusion(bf16[1024,8192]{1,0:T(8,128)(2,1)} %param.6, bf16[8192,256]{1,0:T(8,128)(2,1)} %bitcast), kind=kOutput, calls=%fused_computation | convolution fusion | flops 4295229440 | bytes 21495808 | tf_op jit(solution)/shard_map/dot_general | solution.py:28
  254.6 0.7 dynamic-slice_add_fusion
  (15 shorter events, 0.1 us)
Async XLA Ops:
  7.2 1.0 copy-start
  7.2 185.5 %reduce-scatter.3.cloned.1.call-start = ((), (), s32[]{:S(2)}) async-start(), calls=%async_computation.3 | async-start | bytes 8650752 | tf_op jit(solution)/shard_map/reduce_scatter | solution.py:37
  22.0 0.9 copy-start.6
  22.9 15.3 %copy-start.7 = (s32[20]{0:T(128)S(1)}, s32[20]{0:T(128)}, u32[]{:S(2)}) copy-start(s32[20]{0:T(128)} %param.11) | copy-start | bytes 244
  22.9 169.8 %copy-start.3 = (f32[256,256]{1,0:T(8,128)S(1)}, f32[256,256]{1,0:T(8,128)}, u32[]{:S(2)}) copy-start(f32[256,256]{1,0:T(8,128)} %param.10) | copy-start | bytes 786436
  22.9 169.8 %copy-start.4 = (f32[256,256]{1,0:T(8,128)S(1)}, f32[256,256]{1,0:T(8,128)}, u32[]{:S(2)}) copy-start(f32[256,256]{1,0:T(8,128)} %param.9) | copy-start | bytes 786436
  25.3 217.0 %all-to-all-start = ((bf16[32,256,256]{2,1,0:T(8,128)(2,1)}), bf16[32,256,256]{2,1,0:T(8,128)(2,1)}, u32[]{:S(2)}, u32[]{:S(2)}) async-start(bf16[32,256,256]{2,1,0:T(8,128)(2,1)} %stack.8), calls=%async_computation | async-start | bytes 8388608 | tf_op jit(solution)/shard_map/all_to_all | solution.py:31
  38.1 197.4 %reduce-scatter.5.cloned.1.call-start = ((), (), s32[]{:S(2)}) async-start(), calls=%async_computation.4 | async-start | bytes 2359296 | tf_op jit(solution)/shard_map/reduce_scatter | solution.py:55
  193.7 60.9 %copy-start.1 = (f32[256,256]{1,0:T(8,128)}, f32[256,256]{1,0:T(8,128)S(1)}, u32[]{:S(2)}) copy-start(f32[256,256]{1,0:T(8,128)S(1)} %get-tuple-element.4) | copy-start | bytes 786436
  193.8 60.9 %copy-start.2 = (f32[256,256]{1,0:T(8,128)}, f32[256,256]{1,0:T(8,128)S(1)}, u32[]{:S(2)}) copy-start(f32[256,256]{1,0:T(8,128)S(1)} %get-tuple-element.5) | copy-start | bytes 786436
  236.4 18.2 %collective-permute-start = (f32[4,2,128,32]{2,3,1,0:T(8,128)S(1)}, f32[4,2,128,32]{2,3,1,0:T(8,128)S(1)}, u32[]{:S(2)}, u32[]{:S(2)}) collective-permute-start(f32[4,2,128,32]{2,3,1,0:T(8,128)S(1)} %constant_dynamic-slice_fusion), channel_id=1, source_target_pairs={{0,8},{8,0},{16,24},{24,16},{32,40},{40,32},{48,56},{56,48},{64,72... | collective-permute-start | bytes 393224 | tf_op jit(solution)/shard_map/ppermute | solution.py:13
  242.3 12.3 %copy-start.5 = (f32[4,2,256,32]{2,3,1,0:T(8,128)S(1)}, f32[4,2,256,32]{2,3,1,0:T(8,128)}, u32[]{:S(2)}) copy-start(f32[4,2,256,32]{2,3,1,0:T(8,128)} %reduce-scatter.5.cloned.1.call-done) | copy-start | bytes 786436
Sparse Core Ops, SparseCore 0:
  22.1 170.5 reduce-scatter.2
  195.8 39.7 reduce-scatter.4
